TPU v7x, 256 devices: a whole 4x4x8 slice. The times are simulated.
256 devices in a mesh: view: 2 (over x_hi), seq: 8 (over y, core), event: 16 (over x_lo, z).
Axes of the slice: x: 4 (x_hi: 2, x_lo: 2; x = x_hi * 2 + x_lo), y: 4, z: 8, core: 2. Of those that a mesh axis runs over, the one named last changes fastest.
Arguments:
- query: bfloat16 [16, 2, 3072, 512], P('event', 'view', 'seq'), may hold values from -7 to 7
- key: bfloat16 [16, 2, 3072, 512], P('event', 'view', 'seq'), may hold values from -7 to 7
- value: bfloat16 [16, 2, 3072, 512], P('event', 'view', 'seq'), may hold values from -6 to 6
- pattern: int32 [16, 2, 24, 24], P('event', 'view', 'seq'), may hold values from 0 to 1, as said below
- out_weight: bfloat16 [512, 512], replicated, may hold values from -0.25 to 0.25
- served: int32 [16, 2, 128, 128], P('event', 'view', 'seq'), may hold values from 0 to 383
- anchor_rows: int32 [16, 2, 2048], P('event', 'view', 'seq'), may hold values from 0 to 383
- positive_slot: int32 [16, 2, 2048], P('event', 'view', 'seq'), may hold values from 0 to 2047, as said below
- anchor_live: int32 [16, 2, 2048], P('event', 'view', 'seq'), may hold values from 0 to 1, as said below
Outputs:
- mixed: bfloat16 [16, 2, 3072, 512], P('event', 'view', 'seq')
- grad_wo: float32 [512, 512], replicated
- loss: float32 [], replicated
Inputs may be any that keep to these rules, and one draw needn't show every extreme that they name: pattern[e, v, b, b] is 1 for every block b. `positive_slot`: for an anchor of view v the slot lies in [(1 - v) * 1024, (2 - v) * 1024), a point of the other view. `anchor_live`: every device's block of 256 anchors holds at least one live anchor.
All inputs are finite; a program needn't handle non-finite values.
Results may differ from a plain program's by a relative error of at most 0.015.
Values may be sent and summed in bfloat16 or wider, within the bound.
No kernel may reach another device: no remote copies, remote signals or barrier semaphores. Data moves between devices by JAX's collectives and lax.ppermute only.
A program may use at most 64 MiB of HBM per device.

v0:
```python
import jax
import jax.numpy as jnp
from jax import lax
from jax.sharding import PartitionSpec as P

HEADS = 16
BLOCK = 128
NEGATIVE = -1e30
SHARPNESS_SCALE = 0.07


def from_behind(array, axis, by):
    peers = lax.axis_size(axis)
    return lax.ppermute(array, axis, [(i, (i + by) % peers) for i in range(peers)])


def per_device(
    query, key, value, pattern, out_weight, served, anchor_rows, positive_slot, anchor_live
):
    queries = query[0, 0]
    keys = key[0, 0]
    values = value[0, 0]
    points, width = queries.shape
    head_dim = width // HEADS
    scale = head_dim ** (-0.5)
    loop_size = lax.axis_size("seq")
    myself = lax.axis_index("seq")
    local_pattern = pattern[0, 0].astype(jnp.float32)
    blocks_dev, blocks_all = local_pattern.shape
    query_block = jnp.arange(points) // BLOCK
    pick_rows = (query_block[:, None] == jnp.arange(blocks_dev)[None, :]).astype(jnp.float32)
    row_pattern = jnp.dot(pick_rows, local_pattern, preferred_element_type=jnp.float32)
    head_queries = queries.reshape(points, HEADS, head_dim)

    def attend(state, key_piece, value_piece, start):
        length = key_piece.shape[0]
        count = length // BLOCK
        size = BLOCK
        key_groups = key_piece.reshape(count, size, width)
        value_groups = value_piece.reshape(count, size, width)
        offsets = start + jnp.arange(count, dtype=jnp.int32) * size

        def one_group(carry, inputs):
            key_group, value_group, offset = inputs
            key_block = (offset + jnp.arange(size)) // BLOCK
            pick_keys = (jnp.arange(blocks_all)[:, None] == key_block[None, :]).astype(jnp.float32)
            allowed = jnp.dot(row_pattern, pick_keys, preferred_element_type=jnp.float32) > 0.5
            best, total, accum = carry
            head_keys = key_group.reshape(size, HEADS, head_dim)
            head_values = value_group.reshape(size, HEADS, head_dim)
            scores = (
                jnp.einsum(
                    "qhd,khd->hqk", head_queries, head_keys, preferred_element_type=jnp.float32
                )
                * scale
            )
            scores = jnp.where(allowed[None], scores, NEGATIVE)
            new_best = jnp.maximum(best, jnp.max(scores, axis=-1))
            weights = jnp.where(allowed[None], jnp.exp(scores - new_best[..., None]), 0.0)
            factor = jnp.exp(best - new_best)
            total = total * factor + jnp.sum(weights, axis=-1)
            added = jnp.einsum(
                "hqk,khd->hqd",
                weights.astype(jnp.bfloat16),
                head_values,
                preferred_element_type=jnp.float32,
            )
            result = (new_best, total, accum * factor[..., None] + added)
            return (result, None)

        final_state, unused = lax.scan(one_group, state, (key_groups, value_groups, offsets))
        return final_state

    initial = (
        jnp.full((HEADS, points), NEGATIVE, jnp.float32),
        jnp.zeros((HEADS, points), jnp.float32),
        jnp.zeros((HEADS, points, head_dim), jnp.float32),
    )
    state = attend(initial, keys, values, myself * points)
    moving = (keys, values)
    for step in range(1, loop_size):
        moving = from_behind((moving[0], moving[1]), "seq", 1)
        root = (myself - step) % loop_size
        state = attend(state, moving[0], moving[1], root * points)
    best, total, accum = state
    mixed = (
        (accum / total[..., None]).transpose(1, 0, 2).reshape(points, width).astype(jnp.bfloat16)
    )
    embedding_rows = jnp.dot(mixed, out_weight, preferred_element_type=jnp.float32)
    inverse = lax.rsqrt(jnp.sum(embedding_rows * embedding_rows, axis=-1) + 1e-06)
    unit = (embedding_rows * inverse[:, None]).astype(jnp.bfloat16)
    served_rows = served[0, 0]
    senders, capacity = served_rows.shape
    flat_served = served_rows.reshape(-1)
    outgoing = jnp.take(unit, flat_served, axis=0).reshape(senders, capacity, width)
    incoming = lax.all_to_all(outgoing, ("view", "seq"), split_axis=0, concat_axis=0, tiled=True)
    contender_vectors = incoming.reshape(senders * capacity, width)
    own_rows = anchor_rows[0, 0]
    query_vectors = jnp.take(unit, own_rows, axis=0)
    pairwise_scores = (
        lax.dot_general(
            query_vectors,
            contender_vectors,
            (((1,), (1,)), ((), ())),
            preferred_element_type=jnp.float32,
        )
        / SHARPNESS_SCALE
    )
    exponentiated_scores = jnp.exp(pairwise_scores)
    partition_totals = jnp.sum(exponentiated_scores, axis=-1)
    log_total = jnp.log(partition_totals)
    correct_column = (
        jnp.arange(senders * capacity)[None, :] == positive_slot[0, 0][:, None]
    ).astype(jnp.float32)
    active_queries = anchor_live[0, 0].astype(jnp.float32)
    loss_part = jnp.sum(
        active_queries * (log_total - jnp.sum(pairwise_scores * correct_column, axis=-1))
    )
    live_part = jnp.sum(active_queries)
    score_derivatives = (
        active_queries[:, None]
        * (exponentiated_scores / partition_totals[:, None] - correct_column)
        / SHARPNESS_SCALE
    )
    anchor_grads = jnp.dot(
        score_derivatives, contender_vectors.astype(jnp.float32), precision=lax.Precision.HIGHEST
    )
    candidate_grads = lax.dot_general(
        score_derivatives,
        query_vectors.astype(jnp.float32),
        (((0,), (0,)), ((), ())),
        precision=lax.Precision.HIGHEST,
    )
    returned = lax.all_to_all(
        candidate_grads.reshape(senders, capacity, width).astype(jnp.bfloat16),
        ("view", "seq"),
        split_axis=0,
        concat_axis=0,
        tiled=True,
    ).astype(jnp.float32)
    unit_grads = (
        jnp.zeros((points, width), jnp.float32).at[flat_served].add(returned.reshape(-1, width))
    )
    unit_grads = unit_grads.at[own_rows].add(anchor_grads)
    inner = jnp.sum(embedding_rows * unit_grads, axis=-1)
    embedding_gradients = (
        inverse[:, None] * (unit_grads - embedding_rows * (inverse * inverse * inner)[:, None])
    ).astype(jnp.bfloat16)
    loss_term = lax.dot_general(
        mixed, embedding_gradients, (((0,), (0,)), ((), ())), preferred_element_type=jnp.float32
    )
    grad_total, loss_total, live_total = lax.psum(
        (loss_term, loss_part, live_part), ("view", "seq", "event")
    )
    return (mixed[None, None], grad_total, loss_total / live_total)


def solution(mesh):
    placed = (
        P("event", "view", "seq", None),
        P("event", "view", "seq", None),
        P("event", "view", "seq", None),
        P("event", "view", "seq", None),
        P(),
        P("event", "view", "seq", None),
        P("event", "view", "seq"),
        P("event", "view", "seq"),
        P("event", "view", "seq"),
    )
    return jax.shard_map(
        per_device,
        mesh=mesh,
        in_specs=placed,
        out_specs=(P("event", "view", "seq", None), P(), P()),
        check_vma=False,
    )
```

profile of v0, /device:TPU:2, one launch (start us, length us, event | category | flops | bytes accessed | tf_op | source)
XLA Modules:
  0.0 610.7 jit_solution(11017529696734789384)
XLA Ops:
  7.2 1.7 collective-permute-start.1
  11.1 31.8 %while.136 = (s32[]{:T(128)}, f32[16,384]{1,0:T(8,128)S(1)}, f32[16,384]{1,0:T(8,128)S(1)}, f32[16,384,32]{1,2,0:T(8,128)S(1)}, s32[3]{0:T(128)S(1)}, /*index=5*...) while((s32[]{:T(128)}, f32[16,384]{1,0:T(8,128)S(1)}, ...), condition=%wide.region_3.4_spmd.clone, body=%wide.region_0.3_spmd.clone.sunk | while | flops 113921024 | bytes 13323405 | solution.py:71
  13.7 2.3 fusion.316
  16.0 2.7 fusion.317
  18.8 2.8 fusion.319
  24.3 2.3 fusion.316
  26.6 2.7 fusion.317
  29.4 2.8 fusion.319
  34.9 2.3 fusion.316
  37.2 2.7 fusion.317
  40.0 2.8 fusion.319
  44.8 26.6 %while.129 = (s32[]{:T(128)}, f32[16,384]{1,0:T(8,128)S(1)}, f32[16,384]{1,0:T(8,128)S(1)}, f32[16,384,32]{1,2,0:T(8,128)S(1)}, s32[3]{0:T(128)S(1)}, /*index=5*...) while((s32[]{:T(128)}, f32[16,384]{1,0:T(8,128)S(1)}, ...), condition=%wide.region_7.8_spmd, body=%wide.region_4.7_spmd.sunk | while | flops 113705984 | bytes 25906324 | solution.py:71
  50.8 2.8 fusion.255
  59.7 2.8 fusion.255
  66.0 1.6 copy-done.1
  68.6 2.8 fusion.255
  72.8 26.6 %while.130 = (s32[]{:T(128)}, f32[16,384]{1,0:T(8,128)S(1)}, f32[16,384]{1,0:T(8,128)S(1)}, f32[16,384,32]{1,2,0:T(8,128)S(1)}, s32[3]{0:T(128)S(1)}, /*index=5*...) while((s32[]{:T(128)}, f32[16,384]{1,0:T(8,128)S(1)}, ...), condition=%wide.region_11.12_spmd, body=%wide.region_8.11_spmd.sunk | while | flops 113705984 | bytes 25906324 | solution.py:71
  76.3 1.6 copy-done.2
  78.8 2.8 fusion.264
  85.1 1.6 copy-done.2
  87.7 2.8 fusion.264
  96.6 2.8 fusion.264
  100.0 26.6 %while.131 = (s32[]{:T(128)}, f32[16,384]{1,0:T(8,128)S(1)}, f32[16,384]{1,0:T(8,128)S(1)}, f32[16,384,32]{1,2,0:T(8,128)S(1)}, s32[3]{0:T(128)S(1)}, /*index=5*...) while((s32[]{:T(128)}, f32[16,384]{1,0:T(8,128)S(1)}, ...), condition=%wide.region_15.16_spmd, body=%wide.region_12.15_spmd.sunk | while | flops 113705984 | bytes 25906324 | solution.py:71
  103.4 1.6 copy-done.3
  106.0 2.8 fusion.273
  112.3 1.6 copy-done.3
  114.9 2.8 fusion.273
  123.8 2.8 fusion.273
  128.1 26.6 %while.132 = (s32[]{:T(128)}, f32[16,384]{1,0:T(8,128)S(1)}, f32[16,384]{1,0:T(8,128)S(1)}, f32[16,384,32]{1,2,0:T(8,128)S(1)}, s32[3]{0:T(128)S(1)}, /*index=5*...) while((s32[]{:T(128)}, f32[16,384]{1,0:T(8,128)S(1)}, ...), condition=%wide.region_19.20_spmd, body=%wide.region_16.19_spmd.sunk | while | flops 113705984 | bytes 25906324 | solution.py:71
  134.2 2.8 fusion.282
  140.5 1.6 copy-done.4
  143.0 2.8 fusion.282
  149.3 1.6 copy-done.4
  151.9 2.8 fusion.282
  156.5 26.6 %while.133 = (s32[]{:T(128)}, f32[16,384]{1,0:T(8,128)S(1)}, f32[16,384]{1,0:T(8,128)S(1)}, f32[16,384,32]{1,2,0:T(8,128)S(1)}, s32[3]{0:T(128)S(1)}, /*index=5*...) while((s32[]{:T(128)}, f32[16,384]{1,0:T(8,128)S(1)}, ...), condition=%wide.region_23.24_spmd, body=%wide.region_20.23_spmd.sunk | while | flops 113705984 | bytes 25906324 | solution.py:71
  162.5 2.8 fusion.291
  171.4 2.8 fusion.291
  177.7 1.6 copy-done.5
  180.3 2.8 fusion.291
  184.5 26.0 %while.134 = (s32[]{:T(128)}, f32[16,384]{1,0:T(8,128)S(1)}, f32[16,384]{1,0:T(8,128)S(1)}, f32[16,384,32]{1,2,0:T(8,128)S(1)}, s32[3]{0:T(128)S(1)}, /*index=5*...) while((s32[]{:T(128)}, f32[16,384]{1,0:T(8,128)S(1)}, ...), condition=%wide.region_27.28_spmd, body=%wide.region_24.27_spmd.sunk | while | flops 113705984 | bytes 25906324 | solution.py:71
  187.8 1.6 copy-done.6
  190.3 2.8 fusion.300
  199.0 2.8 fusion.300
  205.1 1.6 copy-done.6
  207.7 2.8 fusion.300
  210.5 23.4 %while.135 = (s32[]{:T(128)}, f32[16,384]{1,0:T(8,128)S(1)}, f32[16,384]{1,0:T(8,128)S(1)}, f32[16,384,32]{1,2,0:T(8,128)S(1)}, s32[3]{0:T(128)S(1)}, /*index=5*...) while((s32[]{:T(128)}, f32[16,384]{1,0:T(8,128)S(1)}, ...), condition=%wide.region_31.32_spmd, body=%wide.region_28.31_spmd.sunk | while | flops 113705984 | bytes 25906324 | solution.py:71
  215.5 2.8 fusion.309
  220.7 1.6 copy-done.7
  223.3 2.8 fusion.309
  231.1 2.8 fusion.309
  234.6 9.2 %gather_fusion.1 = bf16[2048,512]{1,0:T(8,128)(2,1)} fusion(bf16[384,512]{1,0:T(8,128)(2,1)S(1)} %multiply_convert_fusion.1, s32[2048]{0:T(1024)S(1)} %broadcast_clamp_fusion), kind=kCustom, calls=%fused_computation.1 | custom fusion | bytes 4202496 | tf_op jit(solution)/shard_map/jit(_take)/gather | solution.py:95
  243.8 2.7 broadcast_select_fusion
  246.5 5.3 all-to-all-start
  253.1 28.8 %all-to-all-done = bf16[16,128,512]{2,1,0:T(8,128)(2,1)} async-done(((bf16[16,128,512]{2,1,0:T(8,128)(2,1)}), bf16[16,128,512]{2,1,0:T(8,128)(2,1)}, u32[]{:S(2)}, u32[]{:S(2)}) %all-to-all-start) | async-done | bytes 2097184 | tf_op jit(solution)/shard_map/all_to_all | solution.py:96
  281.9 2.6 select_reduce_fusion
  284.5 3.8 convolution_convert_fusion
  288.2 5.7 all-to-all-start.1
  294.0 4.5 fusion.136
  298.4 25.5 %all-to-all-done.1 = bf16[16,128,512]{2,1,0:T(8,128)(2,1)} async-done(((bf16[16,128,512]{2,1,0:T(8,128)(2,1)}), bf16[16,128,512]{2,1,0:T(8,128)(2,1)}, u32[]{:S(2)}, u32[]{:S(2)}) %all-to-all-start.1) | async-done | bytes 2097184 | tf_op jit(solution)/shard_map/all_to_all | solution.py:134
  323.9 13.5 %scatter_custom_fusion = f32[384,512]{1,0:T(8,128)S(1)} fusion(s32[2048]{0:T(1024)} %bitcast.431, bf16[2048,512]{1,0:T(8,128)(2,1)} %bitcast.76, f32[]{:T(128)} %constant.623.clone.1), kind=kCustom, calls=%fused_computation.191 | custom fusion | flops 2097152 | bytes 2884096 | tf_op jit(solution)/shard_map/scatter-add | solution.py:142
  337.5 2.4 scatter_fusion
  343.8 80.3 %all-reduce = (f32[]{:T(128)}, f32[]{:T(128)}) all-reduce(f32[]{:T(128)} %multiply_reduce_fusion.2, f32[]{:T(128)} %convert_reduce_fusion), channel_id=1, replica_groups=mesh['view'=2,'seq'=8,'event'=16] {'view','seq','event'}, use_global_device_ids=true, to_apply=%region_40.41 | all-reduce | flops 2 | bytes 16 | tf_op jit(solution)/shard_map/psum | solution.py:152
  425.5 175.0 %all-reduce.3.cloned.1.call-done = f32[512,512]{1,0:T(8,128)} async-done(((f32[512,512]{1,0:T(8,128)}), f32[512,512]{1,0:T(8,128)}) %all-reduce.3.cloned.1.call-update) | async-done | bytes 1048592 | tf_op jit(solution)/shard_map/psum | solution.py:152
  600.5 2.3 copy.209
  (365 shorter events, 127.9 us)
Async XLA Ops:
  7.2 226.8 %copy-start = (bf16[512,512]{1,0:T(8,128)(2,1)S(1)}, bf16[512,512]{1,0:T(8,128)(2,1)}, u32[]{:S(2)}) copy-start(bf16[512,512]{1,0:T(8,128)(2,1)} %param.29) | copy-start | bytes 1572868
  7.2 35.9 %collective-permute-start = (bf16[384,512]{1,0:T(8,128)(2,1)}, bf16[384,512]{1,0:T(8,128)(2,1)}, u32[]{:S(2)}, u32[]{:S(2)}) collective-permute-start(bf16[384,512]{1,0:T(8,128)(2,1)} %bitcast.423), channel_id=1, source_target_pairs={{0,16},{16,32},{32,48},{48,64},{64,80},{80,96},{96,112},{112,0},{1... | collective-permute-start | bytes 1179656 | tf_op jit(solution)/shard_map/ppermute | solution.py:14
  7.2 36.0 %collective-permute-start.1 = (bf16[384,512]{1,0:T(8,128)(2,1)}, bf16[384,512]{1,0:T(8,128)(2,1)}, u32[]{:S(2)}, u32[]{:S(2)}) collective-permute-start(bf16[384,512]{1,0:T(8,128)(2,1)} %bitcast.425), channel_id=1, source_target_pairs={{0,16},{16,32},{32,48},{48,64},{64,80},{80,96},{96,112},{112,0},{1... | collective-permute-start | bytes 1179656 | tf_op jit(solution)/shard_map/ppermute | solution.py:14
  11.1 31.9 %copy-start.8 = (s32[1,1,16,128]{3,2,1,0:T(8,128)S(1)}, s32[1,1,16,128]{3,2,1,0:T(8,128)}, u32[]{:S(2)}) copy-start(s32[1,1,16,128]{3,2,1,0:T(8,128)} %param.30) | copy-start | bytes 24580
  43.0 1.8 copy-start.9
  43.1 28.3 %collective-permute-start.2 = (bf16[384,512]{1,0:T(8,128)(2,1)}, bf16[384,512]{1,0:T(8,128)(2,1)}, u32[]{:S(2)}, u32[]{:S(2)}) collective-permute-start(bf16[384,512]{1,0:T(8,128)(2,1)} %collective-permute-done), channel_id=1, source_target_pairs={{0,16},{16,32},{32,48},{48,64},{64,80},{80,96},{96,112},{112,0},{1... | collective-permute-start | bytes 1179656 | tf_op jit(solution)/shard_map/ppermute | solution.py:14
  43.2 28.3 %collective-permute-start.3 = (bf16[384,512]{1,0:T(8,128)(2,1)}, bf16[384,512]{1,0:T(8,128)(2,1)}, u32[]{:S(2)}, u32[]{:S(2)}) collective-permute-start(bf16[384,512]{1,0:T(8,128)(2,1)} %collective-permute-done.1), channel_id=1, source_target_pairs={{0,16},{16,32},{32,48},{48,64},{64,80},{80,96},{96,112},{112,0},{1... | collective-permute-start | bytes 1179656 | tf_op jit(solution)/shard_map/ppermute | solution.py:14
  48.2 1.7 copy-start.1
  57.1 1.7 copy-start.1
  66.0 1.7 copy-start.1
  71.4 28.0 %collective-permute-start.4 = (bf16[384,512]{1,0:T(8,128)(2,1)}, bf16[384,512]{1,0:T(8,128)(2,1)}, u32[]{:S(2)}, u32[]{:S(2)}) collective-permute-start(bf16[384,512]{1,0:T(8,128)(2,1)} %collective-permute-done.2), channel_id=1, source_target_pairs={{0,16},{16,32},{32,48},{48,64},{64,80},{80,96},{96,112},{112,0},{1... | collective-permute-start | bytes 1179656 | tf_op jit(solution)/shard_map/ppermute | solution.py:14
  71.5 28.0 %collective-permute-start.5 = (bf16[384,512]{1,0:T(8,128)(2,1)}, bf16[384,512]{1,0:T(8,128)(2,1)}, u32[]{:S(2)}, u32[]{:S(2)}) collective-permute-start(bf16[384,512]{1,0:T(8,128)(2,1)} %collective-permute-done.3), channel_id=1, source_target_pairs={{0,16},{16,32},{32,48},{48,64},{64,80},{80,96},{96,112},{112,0},{1... | collective-permute-start | bytes 1179656 | tf_op jit(solution)/shard_map/ppermute | solution.py:14
  76.2 1.7 copy-start.2
  85.1 1.7 copy-start.2
  94.0 1.7 copy-start.2
  99.4 27.2 %collective-permute-start.6 = (bf16[384,512]{1,0:T(8,128)(2,1)}, bf16[384,512]{1,0:T(8,128)(2,1)}, u32[]{:S(2)}, u32[]{:S(2)}) collective-permute-start(bf16[384,512]{1,0:T(8,128)(2,1)} %collective-permute-done.4), channel_id=1, source_target_pairs={{0,16},{16,32},{32,48},{48,64},{64,80},{80,96},{96,112},{112,0},{1... | collective-permute-start | bytes 1179656 | tf_op jit(solution)/shard_map/ppermute | solution.py:14
  99.6 27.2 %collective-permute-start.7 = (bf16[384,512]{1,0:T(8,128)(2,1)}, bf16[384,512]{1,0:T(8,128)(2,1)}, u32[]{:S(2)}, u32[]{:S(2)}) collective-permute-start(bf16[384,512]{1,0:T(8,128)(2,1)} %collective-permute-done.5), channel_id=1, source_target_pairs={{0,16},{16,32},{32,48},{48,64},{64,80},{80,96},{96,112},{112,0},{1... | collective-permute-start | bytes 1179656 | tf_op jit(solution)/shard_map/ppermute | solution.py:14
  103.4 1.7 copy-start.3
  112.3 1.7 copy-start.3
  121.2 1.7 copy-start.3
  126.6 28.1 %collective-permute-start.8 = (bf16[384,512]{1,0:T(8,128)(2,1)}, bf16[384,512]{1,0:T(8,128)(2,1)}, u32[]{:S(2)}, u32[]{:S(2)}) collective-permute-start(bf16[384,512]{1,0:T(8,128)(2,1)} %collective-permute-done.6), channel_id=1, source_target_pairs={{0,16},{16,32},{32,48},{48,64},{64,80},{80,96},{96,112},{112,0},{1... | collective-permute-start | bytes 1179656 | tf_op jit(solution)/shard_map/ppermute | solution.py:14
  126.8 28.1 %collective-permute-start.9 = (bf16[384,512]{1,0:T(8,128)(2,1)}, bf16[384,512]{1,0:T(8,128)(2,1)}, u32[]{:S(2)}, u32[]{:S(2)}) collective-permute-start(bf16[384,512]{1,0:T(8,128)(2,1)} %collective-permute-done.7), channel_id=1, source_target_pairs={{0,16},{16,32},{32,48},{48,64},{64,80},{80,96},{96,112},{112,0},{1... | collective-permute-start | bytes 1179656 | tf_op jit(solution)/shard_map/ppermute | solution.py:14
  131.6 1.7 copy-start.4
  140.4 1.7 copy-start.4
  149.3 1.7 copy-start.4
  154.8 28.3 %collective-permute-start.10 = (bf16[384,512]{1,0:T(8,128)(2,1)}, bf16[384,512]{1,0:T(8,128)(2,1)}, u32[]{:S(2)}, u32[]{:S(2)}) collective-permute-start(bf16[384,512]{1,0:T(8,128)(2,1)} %collective-permute-done.8), channel_id=1, source_target_pairs={{0,16},{16,32},{32,48},{48,64},{64,80},{80,96},{96,112},{112,0},{1... | collective-permute-start | bytes 1179656 | tf_op jit(solution)/shard_map/ppermute | solution.py:14
  154.9 28.3 %collective-permute-start.11 = (bf16[384,512]{1,0:T(8,128)(2,1)}, bf16[384,512]{1,0:T(8,128)(2,1)}, u32[]{:S(2)}, u32[]{:S(2)}) collective-permute-start(bf16[384,512]{1,0:T(8,128)(2,1)} %collective-permute-done.9), channel_id=1, source_target_pairs={{0,16},{16,32},{32,48},{48,64},{64,80},{80,96},{96,112},{112,0},{1... | collective-permute-start | bytes 1179656 | tf_op jit(solution)/shard_map/ppermute | solution.py:14
  159.9 1.7 copy-start.5
  168.8 1.7 copy-start.5
  177.6 1.7 copy-start.5
  183.1 27.4 %collective-permute-start.12 = (bf16[384,512]{1,0:T(8,128)(2,1)}, bf16[384,512]{1,0:T(8,128)(2,1)S(1)}, u32[]{:S(2)}, u32[]{:S(2)}) collective-permute-start(bf16[384,512]{1,0:T(8,128)(2,1)} %collective-permute-done.10), channel_id=1, source_target_pairs={{0,16},{16,32},{32,48},{48,64},{64,80},{80,96},{96,112},{112,0},{1... | collective-permute-start | bytes 1179656 | tf_op jit(solution)/shard_map/ppermute | solution.py:14
  183.2 27.3 %collective-permute-start.13 = (bf16[384,512]{1,0:T(8,128)(2,1)}, bf16[384,512]{1,0:T(8,128)(2,1)S(1)}, u32[]{:S(2)}, u32[]{:S(2)}) collective-permute-start(bf16[384,512]{1,0:T(8,128)(2,1)} %collective-permute-done.11), channel_id=1, source_target_pairs={{0,16},{16,32},{32,48},{48,64},{64,80},{80,96},{96,112},{112,0},{1... | collective-permute-start | bytes 1179656 | tf_op jit(solution)/shard_map/ppermute | solution.py:14
  187.7 1.7 copy-start.6
  196.4 1.7 copy-start.6
  205.1 1.7 copy-start.6
  212.9 1.7 copy-start.7
  220.7 1.7 copy-start.7
  228.5 1.7 copy-start.7
  246.5 5.3 copy-start.11
  246.5 5.3 copy-start.10
  246.5 35.3 %copy-start.12 = (s32[1,1,256]{2,1,0:T(1,128)S(1)}, s32[1,1,256]{2,1,0:T(1,128)}, u32[]{:S(2)}) copy-start(s32[1,1,256]{2,1,0:T(1,128)} %param.32) | copy-start | bytes 3076
  246.5 35.3 %all-to-all-start = ((bf16[16,128,512]{2,1,0:T(8,128)(2,1)}), bf16[16,128,512]{2,1,0:T(8,128)(2,1)}, u32[]{:S(2)}, u32[]{:S(2)}) async-start(bf16[16,128,512]{2,1,0:T(8,128)(2,1)} %broadcast_select_fusion), calls=%async_computation | async-start | bytes 4194304 | tf_op jit(solution)/shard_map/all_to_all | solution.py:96
  284.5 3.8 copy-start.13
  288.2 35.7 %all-to-all-start.1 = ((bf16[16,128,512]{2,1,0:T(8,128)(2,1)}), bf16[16,128,512]{2,1,0:T(8,128)(2,1)}, u32[]{:S(2)}, u32[]{:S(2)}) async-start(bf16[16,128,512]{2,1,0:T(8,128)(2,1)} %bitcast.422), calls=%async_computation.1 | async-start | bytes 4194304 | tf_op jit(solution)/shard_map/all_to_all | solution.py:134
  293.9 306.5 %all-reduce.3.cloned.1.call-start = ((), (), s32[]{:S(2)}) async-start(), calls=%async_computation.2 | async-start | bytes 2097152 | tf_op jit(solution)/shard_map/psum | solution.py:152
Sparse Core Ops, SparseCore 0:
  341.7 258.7 all-reduce.2
where the time goes:
time: 613 us; the launch traced here: 611 us
  waiting for transfers between devices  229 us (37%)
  matrix products  108 us (18%)
  local copies, waits for them, and re-layouts  91.3 us (15%)
  blocking collectives  80.3 us (13%)
  other arithmetic  62.2 us (10%)
  starting transfers between devices  21 us (3%)
  between operations  17 us (3%)
    psum x1, waiting for transfers between devices, per_device(): lax.psum((loss_term, loss_part, live_part), ('view', 'seq', 'event'))  175 us
    psum x1, blocking collectives, per_device(): lax.psum((loss_term, loss_part, live_part), ('view', 'seq', 'event'))  80.3 us
    dot_general x24, matrix products, one_group(): jnp.einsum('hqk,khd->hqd', weights.astype(jnp.bfloat16), head_values, pre...  67.5 us
    dynamic_slice x96, local copies, waits for them, and re-layouts, attend(): lax.scan(one_group, state, (key_groups, value_groups, offsets))  41.9 us
    while x66, local copies, waits for them, and re-layouts  34.6 us
    all_to_all x1, waiting for transfers between devices, per_device(): lax.all_to_all(outgoing, ('view', 'seq'), split_axis=0, concat_axis=0, ti...  28.8 us
    all_to_all x1, waiting for transfers between devices, per_device(): lax.all_to_all(candidate_grads.reshape(senders, capacity, width).astype(j...  25.5 us
    reduce_sum x24, other arithmetic, one_group(): total = total * factor + jnp.sum(weights, axis=-1)  24.6 us
  transfers between devices with their start and end apart: 17, of which 3 were waited for; matrix products, arithmetic and copies ran while one was open for 28% of the time, Pallas kernels for 0%

commit v1 on v0

--- a/solution.py
+++ b/solution.py
@@ -150,7 +150,7 @@
         mixed, embedding_gradients, (((0,), (0,)), ((), ())), preferred_element_type=jnp.float32
     )
     grad_total, loss_total, live_total = lax.psum(
-        (loss_term, loss_part, live_part), ("view", "seq", "event")
+        lax.psum((loss_term, loss_part, live_part), axis_name=("seq", "event")), axis_name="view"
     )
     return (mixed[None, None], grad_total, loss_total / live_total)
 

time: 613 us -> 1730 us (2.82)
  waiting for transfers between devices: 229 us -> 1130 us
  blocking collectives: 80.3 us -> 284 us
    psum x1 -> x2, waiting for transfers between devices: 175 us -> 1080 us  [the longest x1 1080 us: per_device(): lax.psum((loss_term, loss_part, live_part), axis_name=('seq', 'event'))]
    psum x1 -> x2, blocking collectives: 80.3 us -> 284 us  [the longest x1 277 us: per_device(): lax.psum((loss_term, loss_part, live_part), axis_name=('seq', 'event'))]
  transfers between devices with their start and end apart: 17 -> 18, of which waited for: 3 -> 3; matrix products, arithmetic and copies ran while one was open for 28% -> 10% of each run, Pallas kernels for 0% -> 0%
where the time goes in v1:
time: 1730 us; the launch traced here: 1720 us
  waiting for transfers between devices  1130 us (65%)
  blocking collectives  284 us (16%)
  matrix products  108 us (6%)
  local copies, waits for them, and re-layouts  92.1 us (5%)
  other arithmetic  63.2 us (4%)
  starting transfers between devices  20.9 us (1%)
    psum x1, waiting for transfers between devices, per_device(): lax.psum((loss_term, loss_part, live_part), axis_name=('seq', 'event'))  1080 us
    psum x1, blocking collectives, per_device(): lax.psum((loss_term, loss_part, live_part), axis_name=('seq', 'event'))  277 us
    dot_general x24, matrix products, one_group(): jnp.einsum('hqk,khd->hqd', weights.astype(jnp.bfloat16), head_values, pre...  67.5 us
    dynamic_slice x96, local copies, waits for them, and re-layouts, attend(): lax.scan(one_group, state, (key_groups, value_groups, offsets))  41.9 us
    while x66, local copies, waits for them, and re-layouts  34.6 us
  transfers between devices with their start and end apart: 18, of which 3 were waited for; matrix products, arithmetic and copies ran while one was open for 10% of the time, Pallas kernels for 0%

profile of v1, /device:TPU:2, one launch (start us, length us, event | category | flops | bytes accessed | tf_op | source)
XLA Modules:
  0.0 1719.3 jit_solution(8709646150008572913)
XLA Ops:
  7.2 1.7 collective-permute-start.1
  11.1 31.8 %while.136 = (s32[]{:T(128)}, f32[16,384]{1,0:T(8,128)S(1)}, f32[16,384]{1,0:T(8,128)S(1)}, f32[16,384,32]{1,2,0:T(8,128)S(1)}, s32[3]{0:T(128)S(1)}, /*index=5*...) while((s32[]{:T(128)}, f32[16,384]{1,0:T(8,128)S(1)}, ...), condition=%wide.region_3.4_spmd.clone, body=%wide.region_0.3_spmd.clone.sunk | while | flops 113921024 | bytes 13323405 | solution.py:71
  13.7 2.3 fusion.316
  16.0 2.7 fusion.317
  18.8 2.8 fusion.319
  24.3 2.3 fusion.316
  26.6 2.7 fusion.317
  29.4 2.8 fusion.319
  34.9 2.3 fusion.316
  37.2 2.7 fusion.317
  40.0 2.8 fusion.319
  44.8 26.6 %while.129 = (s32[]{:T(128)}, f32[16,384]{1,0:T(8,128)S(1)}, f32[16,384]{1,0:T(8,128)S(1)}, f32[16,384,32]{1,2,0:T(8,128)S(1)}, s32[3]{0:T(128)S(1)}, /*index=5*...) while((s32[]{:T(128)}, f32[16,384]{1,0:T(8,128)S(1)}, ...), condition=%wide.region_7.8_spmd, body=%wide.region_4.7_spmd.sunk | while | flops 113705984 | bytes 25906324 | solution.py:71
  50.8 2.8 fusion.255
  57.1 1.6 copy-done.1
  59.7 2.8 fusion.255
  68.6 2.8 fusion.255
  72.8 26.6 %while.130 = (s32[]{:T(128)}, f32[16,384]{1,0:T(8,128)S(1)}, f32[16,384]{1,0:T(8,128)S(1)}, f32[16,384,32]{1,2,0:T(8,128)S(1)}, s32[3]{0:T(128)S(1)}, /*index=5*...) while((s32[]{:T(128)}, f32[16,384]{1,0:T(8,128)S(1)}, ...), condition=%wide.region_11.12_spmd, body=%wide.region_8.11_spmd.sunk | while | flops 113705984 | bytes 25906324 | solution.py:71
  78.8 2.8 fusion.264
  85.1 1.6 copy-done.2
  87.7 2.8 fusion.264
  94.0 1.6 copy-done.2
  96.6 2.8 fusion.264
  100.0 26.6 %while.131 = (s32[]{:T(128)}, f32[16,384]{1,0:T(8,128)S(1)}, f32[16,384]{1,0:T(8,128)S(1)}, f32[16,384,32]{1,2,0:T(8,128)S(1)}, s32[3]{0:T(128)S(1)}, /*index=5*...) while((s32[]{:T(128)}, f32[16,384]{1,0:T(8,128)S(1)}, ...), condition=%wide.region_15.16_spmd, body=%wide.region_12.15_spmd.sunk | while | flops 113705984 | bytes 25906324 | solution.py:71
  103.4 1.6 copy-done.3
  106.0 2.8 fusion.273
  112.3 1.6 copy-done.3
  114.9 2.8 fusion.273
  123.8 2.8 fusion.273
  128.1 26.6 %while.132 = (s32[]{:T(128)}, f32[16,384]{1,0:T(8,128)S(1)}, f32[16,384]{1,0:T(8,128)S(1)}, f32[16,384,32]{1,2,0:T(8,128)S(1)}, s32[3]{0:T(128)S(1)}, /*index=5*...) while((s32[]{:T(128)}, f32[16,384]{1,0:T(8,128)S(1)}, ...), condition=%wide.region_19.20_spmd, body=%wide.region_16.19_spmd.sunk | while | flops 113705984 | bytes 25906324 | solution.py:71
  134.2 2.8 fusion.282
  143.0 2.8 fusion.282
  149.3 1.6 copy-done.4
  151.9 2.8 fusion.282
  156.5 26.6 %while.133 = (s32[]{:T(128)}, f32[16,384]{1,0:T(8,128)S(1)}, f32[16,384]{1,0:T(8,128)S(1)}, f32[16,384,32]{1,2,0:T(8,128)S(1)}, s32[3]{0:T(128)S(1)}, /*index=5*...) while((s32[]{:T(128)}, f32[16,384]{1,0:T(8,128)S(1)}, ...), condition=%wide.region_23.24_spmd, body=%wide.region_20.23_spmd.sunk | while | flops 113705984 | bytes 25906324 | solution.py:71
  162.5 2.8 fusion.291
  168.8 1.6 copy-done.5
  171.4 2.8 fusion.291
  177.7 1.6 copy-done.5
  180.2 2.8 fusion.291
  184.5 26.0 %while.134 = (s32[]{:T(128)}, f32[16,384]{1,0:T(8,128)S(1)}, f32[16,384]{1,0:T(8,128)S(1)}, f32[16,384,32]{1,2,0:T(8,128)S(1)}, s32[3]{0:T(128)S(1)}, /*index=5*...) while((s32[]{:T(128)}, f32[16,384]{1,0:T(8,128)S(1)}, ...), condition=%wide.region_27.28_spmd, body=%wide.region_24.27_spmd.sunk | while | flops 113705984 | bytes 25906324 | solution.py:71
  187.7 1.6 copy-done.6
  190.3 2.8 fusion.300
  199.0 2.8 fusion.300
  207.6 2.8 fusion.300
  210.5 23.4 %while.135 = (s32[]{:T(128)}, f32[16,384]{1,0:T(8,128)S(1)}, f32[16,384]{1,0:T(8,128)S(1)}, f32[16,384,32]{1,2,0:T(8,128)S(1)}, s32[3]{0:T(128)S(1)}, /*index=5*...) while((s32[]{:T(128)}, f32[16,384]{1,0:T(8,128)S(1)}, ...), condition=%wide.region_31.32_spmd, body=%wide.region_28.31_spmd.sunk | while | flops 113705984 | bytes 25906324 | solution.py:71
  212.9 1.6 copy-done.7
  215.5 2.8 fusion.309
  223.2 2.8 fusion.309
  231.0 2.8 fusion.309
  236.6 9.2 gather_fusion.1
  245.8 2.7 broadcast_select_fusion
  248.5 5.2 all-to-all-start
  254.9 28.8 %all-to-all-done = bf16[16,128,512]{2,1,0:T(8,128)(2,1)} async-done(((bf16[16,128,512]{2,1,0:T(8,128)(2,1)}), bf16[16,128,512]{2,1,0:T(8,128)(2,1)}, u32[]{:S(2)}, u32[]{:S(2)}) %all-to-all-start) | async-done | bytes 2097184 | tf_op jit(solution)/shard_map/all_to_all | solution.py:96
  283.7 2.6 select_reduce_fusion
  286.3 3.8 convolution_convert_fusion
  290.1 5.7 all-to-all-start.1
  295.8 4.5 fusion.136
  300.3 25.5 %all-to-all-done.1 = bf16[16,128,512]{2,1,0:T(8,128)(2,1)} async-done(((bf16[16,128,512]{2,1,0:T(8,128)(2,1)}), bf16[16,128,512]{2,1,0:T(8,128)(2,1)}, u32[]{:S(2)}, u32[]{:S(2)}) %all-to-all-start.1) | async-done | bytes 2097184 | tf_op jit(solution)/shard_map/all_to_all | solution.py:134
  325.8 13.5 scatter_custom_fusion
  339.3 2.4 scatter_fusion
  343.5 1078.2 %all-reduce.5.cloned.1.call-done = f32[512,512]{1,0:T(8,128)} async-done(((f32[512,512]{1,0:T(8,128)}), f32[512,512]{1,0:T(8,128)}) %all-reduce.5.cloned.1.call-update) | async-done | bytes 1048592 | tf_op jit(solution)/shard_map/psum | solution.py:153
  1423.9 276.8 %all-reduce = (f32[]{:T(128)}, f32[]{:T(128)}) all-reduce(f32[]{:T(128)} %multiply_reduce_fusion.2, f32[]{:T(128)} %convert_reduce_fusion), channel_id=1, replica_groups=mesh['view'=2,'seq'=8,'event'=16] {'seq','event'}, use_global_device_ids=true, to_apply=%region_41.42 | all-reduce | flops 2 | bytes 16 | tf_op jit(solution)/shard_map/psum | solution.py:153
  1700.7 7.1 all-reduce.1
  1709.1 2.3 copy.210
  (371 shorter events, 131.6 us)
Async XLA Ops:
  7.2 228.8 %copy-start = (bf16[512,512]{1,0:T(8,128)(2,1)S(1)}, bf16[512,512]{1,0:T(8,128)(2,1)}, u32[]{:S(2)}) copy-start(bf16[512,512]{1,0:T(8,128)(2,1)} %param.29) | copy-start | bytes 1572868
  7.2 35.9 %collective-permute-start = (bf16[384,512]{1,0:T(8,128)(2,1)}, bf16[384,512]{1,0:T(8,128)(2,1)}, u32[]{:S(2)}, u32[]{:S(2)}) collective-permute-start(bf16[384,512]{1,0:T(8,128)(2,1)} %bitcast.423), channel_id=1, source_target_pairs={{0,16},{16,32},{32,48},{48,64},{64,80},{80,96},{96,112},{112,0},{1... | collective-permute-start | bytes 1179656 | tf_op jit(solution)/shard_map/ppermute | solution.py:14
  7.2 36.0 %collective-permute-start.1 = (bf16[384,512]{1,0:T(8,128)(2,1)}, bf16[384,512]{1,0:T(8,128)(2,1)}, u32[]{:S(2)}, u32[]{:S(2)}) collective-permute-start(bf16[384,512]{1,0:T(8,128)(2,1)} %bitcast.425), channel_id=1, source_target_pairs={{0,16},{16,32},{32,48},{48,64},{64,80},{80,96},{96,112},{112,0},{1... | collective-permute-start | bytes 1179656 | tf_op jit(solution)/shard_map/ppermute | solution.py:14
  11.1 31.9 %copy-start.9 = (s32[1,1,16,128]{3,2,1,0:T(8,128)S(1)}, s32[1,1,16,128]{3,2,1,0:T(8,128)}, u32[]{:S(2)}) copy-start(s32[1,1,16,128]{3,2,1,0:T(8,128)} %param.30) | copy-start | bytes 24580
  43.0 1.8 copy-start.10
  43.1 28.3 %collective-permute-start.2 = (bf16[384,512]{1,0:T(8,128)(2,1)}, bf16[384,512]{1,0:T(8,128)(2,1)}, u32[]{:S(2)}, u32[]{:S(2)}) collective-permute-start(bf16[384,512]{1,0:T(8,128)(2,1)} %collective-permute-done), channel_id=1, source_target_pairs={{0,16},{16,32},{32,48},{48,64},{64,80},{80,96},{96,112},{112,0},{1... | collective-permute-start | bytes 1179656 | tf_op jit(solution)/shard_map/ppermute | solution.py:14
  43.2 28.3 %collective-permute-start.3 = (bf16[384,512]{1,0:T(8,128)(2,1)}, bf16[384,512]{1,0:T(8,128)(2,1)}, u32[]{:S(2)}, u32[]{:S(2)}) collective-permute-start(bf16[384,512]{1,0:T(8,128)(2,1)} %collective-permute-done.1), channel_id=1, source_target_pairs={{0,16},{16,32},{32,48},{48,64},{64,80},{80,96},{96,112},{112,0},{1... | collective-permute-start | bytes 1179656 | tf_op jit(solution)/shard_map/ppermute | solution.py:14
  48.2 1.7 copy-start.1
  57.1 1.7 copy-start.1
  65.9 1.7 copy-start.1
  71.4 28.0 %collective-permute-start.4 = (bf16[384,512]{1,0:T(8,128)(2,1)}, bf16[384,512]{1,0:T(8,128)(2,1)}, u32[]{:S(2)}, u32[]{:S(2)}) collective-permute-start(bf16[384,512]{1,0:T(8,128)(2,1)} %collective-permute-done.2), channel_id=1, source_target_pairs={{0,16},{16,32},{32,48},{48,64},{64,80},{80,96},{96,112},{112,0},{1... | collective-permute-start | bytes 1179656 | tf_op jit(solution)/shard_map/ppermute | solution.py:14
  71.5 28.0 %collective-permute-start.5 = (bf16[384,512]{1,0:T(8,128)(2,1)}, bf16[384,512]{1,0:T(8,128)(2,1)}, u32[]{:S(2)}, u32[]{:S(2)}) collective-permute-start(bf16[384,512]{1,0:T(8,128)(2,1)} %collective-permute-done.3), channel_id=1, source_target_pairs={{0,16},{16,32},{32,48},{48,64},{64,80},{80,96},{96,112},{112,0},{1... | collective-permute-start | bytes 1179656 | tf_op jit(solution)/shard_map/ppermute | solution.py:14
  76.2 1.7 copy-start.2
  85.1 1.7 copy-start.2
  94.0 1.7 copy-start.2
  99.4 27.2 %collective-permute-start.6 = (bf16[384,512]{1,0:T(8,128)(2,1)}, bf16[384,512]{1,0:T(8,128)(2,1)}, u32[]{:S(2)}, u32[]{:S(2)}) collective-permute-start(bf16[384,512]{1,0:T(8,128)(2,1)} %collective-permute-done.4), channel_id=1, source_target_pairs={{0,16},{16,32},{32,48},{48,64},{64,80},{80,96},{96,112},{112,0},{1... | collective-permute-start | bytes 1179656 | tf_op jit(solution)/shard_map/ppermute | solution.py:14
  99.6 27.2 %collective-permute-start.7 = (bf16[384,512]{1,0:T(8,128)(2,1)}, bf16[384,512]{1,0:T(8,128)(2,1)}, u32[]{:S(2)}, u32[]{:S(2)}) collective-permute-start(bf16[384,512]{1,0:T(8,128)(2,1)} %collective-permute-done.5), channel_id=1, source_target_pairs={{0,16},{16,32},{32,48},{48,64},{64,80},{80,96},{96,112},{112,0},{1... | collective-permute-start | bytes 1179656 | tf_op jit(solution)/shard_map/ppermute | solution.py:14
  103.4 1.7 copy-start.3
  112.3 1.7 copy-start.3
  121.2 1.7 copy-start.3
  126.6 28.1 %collective-permute-start.8 = (bf16[384,512]{1,0:T(8,128)(2,1)}, bf16[384,512]{1,0:T(8,128)(2,1)}, u32[]{:S(2)}, u32[]{:S(2)}) collective-permute-start(bf16[384,512]{1,0:T(8,128)(2,1)} %collective-permute-done.6), channel_id=1, source_target_pairs={{0,16},{16,32},{32,48},{48,64},{64,80},{80,96},{96,112},{112,0},{1... | collective-permute-start | bytes 1179656 | tf_op jit(solution)/shard_map/ppermute | solution.py:14
  126.7 28.1 %collective-permute-start.9 = (bf16[384,512]{1,0:T(8,128)(2,1)}, bf16[384,512]{1,0:T(8,128)(2,1)}, u32[]{:S(2)}, u32[]{:S(2)}) collective-permute-start(bf16[384,512]{1,0:T(8,128)(2,1)} %collective-permute-done.7), channel_id=1, source_target_pairs={{0,16},{16,32},{32,48},{48,64},{64,80},{80,96},{96,112},{112,0},{1... | collective-permute-start | bytes 1179656 | tf_op jit(solution)/shard_map/ppermute | solution.py:14
  131.5 1.7 copy-start.4
  140.4 1.7 copy-start.4
  149.3 1.7 copy-start.4
  154.8 28.3 %collective-permute-start.10 = (bf16[384,512]{1,0:T(8,128)(2,1)}, bf16[384,512]{1,0:T(8,128)(2,1)}, u32[]{:S(2)}, u32[]{:S(2)}) collective-permute-start(bf16[384,512]{1,0:T(8,128)(2,1)} %collective-permute-done.8), channel_id=1, source_target_pairs={{0,16},{16,32},{32,48},{48,64},{64,80},{80,96},{96,112},{112,0},{1... | collective-permute-start | bytes 1179656 | tf_op jit(solution)/shard_map/ppermute | solution.py:14
  154.9 28.3 %collective-permute-start.11 = (bf16[384,512]{1,0:T(8,128)(2,1)}, bf16[384,512]{1,0:T(8,128)(2,1)}, u32[]{:S(2)}, u32[]{:S(2)}) collective-permute-start(bf16[384,512]{1,0:T(8,128)(2,1)} %collective-permute-done.9), channel_id=1, source_target_pairs={{0,16},{16,32},{32,48},{48,64},{64,80},{80,96},{96,112},{112,0},{1... | collective-permute-start | bytes 1179656 | tf_op jit(solution)/shard_map/ppermute | solution.py:14
  159.9 1.7 copy-start.5
  168.8 1.7 copy-start.5
  177.6 1.7 copy-start.5
  183.1 27.4 %collective-permute-start.12 = (bf16[384,512]{1,0:T(8,128)(2,1)}, bf16[384,512]{1,0:T(8,128)(2,1)S(1)}, u32[]{:S(2)}, u32[]{:S(2)}) collective-permute-start(bf16[384,512]{1,0:T(8,128)(2,1)} %collective-permute-done.10), channel_id=1, source_target_pairs={{0,16},{16,32},{32,48},{48,64},{64,80},{80,96},{96,112},{112,0},{1... | collective-permute-start | bytes 1179656 | tf_op jit(solution)/shard_map/ppermute | solution.py:14
  183.2 27.3 %collective-permute-start.13 = (bf16[384,512]{1,0:T(8,128)(2,1)}, bf16[384,512]{1,0:T(8,128)(2,1)S(1)}, u32[]{:S(2)}, u32[]{:S(2)}) collective-permute-start(bf16[384,512]{1,0:T(8,128)(2,1)} %collective-permute-done.11), channel_id=1, source_target_pairs={{0,16},{16,32},{32,48},{48,64},{64,80},{80,96},{96,112},{112,0},{1... | collective-permute-start | bytes 1179656 | tf_op jit(solution)/shard_map/ppermute | solution.py:14
  187.7 1.7 copy-start.6
  196.4 1.7 copy-start.6
  205.0 1.7 copy-start.6
  212.8 1.7 copy-start.7
  220.6 1.7 copy-start.7
  228.4 1.7 copy-start.7
  233.9 0.9 copy-start.8
  248.5 5.2 copy-start.12
  248.5 5.2 copy-start.11
  248.5 35.2 %copy-start.13 = (s32[1,1,256]{2,1,0:T(1,128)S(1)}, s32[1,1,256]{2,1,0:T(1,128)}, u32[]{:S(2)}) copy-start(s32[1,1,256]{2,1,0:T(1,128)} %param.32) | copy-start | bytes 3076
  248.5 35.2 %all-to-all-start = ((bf16[16,128,512]{2,1,0:T(8,128)(2,1)}), bf16[16,128,512]{2,1,0:T(8,128)(2,1)}, u32[]{:S(2)}, u32[]{:S(2)}) async-start(bf16[16,128,512]{2,1,0:T(8,128)(2,1)} %broadcast_select_fusion), calls=%async_computation | async-start | bytes 4194304 | tf_op jit(solution)/shard_map/all_to_all | solution.py:96
  286.3 3.8 copy-start.14
  290.1 35.7 %all-to-all-start.1 = ((bf16[16,128,512]{2,1,0:T(8,128)(2,1)}), bf16[16,128,512]{2,1,0:T(8,128)(2,1)}, u32[]{:S(2)}, u32[]{:S(2)}) async-start(bf16[16,128,512]{2,1,0:T(8,128)(2,1)} %bitcast.422), calls=%async_computation.1 | async-start | bytes 4194304 | tf_op jit(solution)/shard_map/all_to_all | solution.py:134
  295.8 1125.9 %all-reduce.5.cloned.1.call-start = ((), (), s32[]{:S(2)}) async-start(), calls=%async_computation.2 | async-start | bytes 2097152 | tf_op jit(solution)/shard_map/psum | solution.py:153
  343.4 1365.7 %all-reduce.7.cloned.1.call-start = ((), (), s32[]{:S(2)}) async-start(), calls=%async_computation.3 | async-start | bytes 2097152 | tf_op jit(solution)/shard_map/psum | solution.py:152
Sparse Core Ops, SparseCore 0:
  343.5 1078.1 all-reduce.4
  1424.5 56.7 all-reduce.6
